TPU v7x, 32 devices: a whole 2x2x4 slice. The times are simulated.
32 devices in a mesh: dp: 8 (over z, y), space: 4 (over x, core).
Axes of the slice: x: 2, y: 2, z: 4, core: 2. Of those that a mesh axis runs over, the one named last changes fastest.
Arguments:
- volume: bfloat16 [8, 4, 32, 32, 32], P('dp', None, 'space'), may hold values from -6 to 6
- cotangent: bfloat16 [8, 64, 512], P('dp', None, 'space'), may hold values from -6 to 6
- conv_one: bfloat16 [32, 4, 3, 3, 3], replicated, may hold values from -0.625 to 0.625
- conv_two: bfloat16 [64, 32, 3, 3, 3], replicated, may hold values from -0.21875 to 0.21875
Outputs:
- out_two: bfloat16 [8, 64, 512], P('dp', None, 'space')
- grad_pre: bfloat16 [8, 32, 4096], P('dp', None, 'space')
- update_one: float32 [3456], replicated
- update_two: float32 [55296], replicated
All inputs are finite; a program needn't handle non-finite values.
Results may differ from a plain program's by a relative error of at most 0.0057.
Values may be sent and summed in bfloat16 or wider, within the bound.
A program may use at most 64 MiB of HBM per device.

v0:
```python
import jax
import jax.numpy as jnp
from jax import lax
from jax.sharding import PartitionSpec as P

damp_input = 0.1
damp_grad = 0.03


def passed_along(value, axis, steps):
    count = lax.axis_size(axis)
    leading, last = (max(0, -steps), min(count, count - steps))
    return lax.ppermute(value, axis, [(source, source + steps) for source in range(leading, last)])


def tap_stack(padded, out_depth, out_rows, out_cols):
    pieces = []
    for depth_tap in range(3):
        for row_tap in range(3):
            for col_tap in range(3):
                pieces.append(
                    padded[
                        :,
                        depth_tap : depth_tap + 2 * out_depth : 2,
                        row_tap : row_tap + 2 * out_rows : 2,
                        col_tap : col_tap + 2 * out_cols : 2,
                    ]
                )
    stacked = jnp.stack(pieces, axis=1)
    return stacked.reshape(stacked.shape[0] * 27, -1)


def spread_taps(columns, channels, out_depth, out_rows, out_cols):
    pieces = columns.reshape(channels, 27, out_depth, out_rows, out_cols)
    canvas = jnp.zeros(
        (channels, 2 * out_depth + 1, 2 * out_rows + 1, 2 * out_cols + 1), jnp.float32
    )
    for depth_tap in range(3):
        for row_tap in range(3):
            for col_tap in range(3):
                tap_number = depth_tap * 9 + row_tap * 3 + col_tap
                canvas = canvas.at[
                    :,
                    depth_tap : depth_tap + 2 * out_depth : 2,
                    row_tap : row_tap + 2 * out_rows : 2,
                    col_tap : col_tap + 2 * out_cols : 2,
                ].add(pieces[:, tap_number])
    return canvas


def silu_slope(pre_act):
    sigmoid_val = jax.nn.sigmoid(pre_act)
    return sigmoid_val * (1.0 + pre_act * (1.0 - sigmoid_val))


def damped_solve(matrix, rhs_terms):
    lower_factor = jnp.linalg.cholesky(matrix)
    return jax.scipy.linalg.cho_solve((lower_factor, True), rhs_terms)


def precondition(gram_in, gram_out, grad_sum, total_rows):
    in_mat = gram_in / total_rows + damp_input * jnp.eye(gram_in.shape[0], dtype=jnp.float32)
    out_mat = gram_out / total_rows + damp_grad * jnp.eye(gram_out.shape[0], dtype=jnp.float32)
    mean_grad = grad_sum / total_rows
    half_solved = damped_solve(in_mat, mean_grad.T).T
    return (damped_solve(out_mat, half_solved), mean_grad)


def on_device(volume, cotangent, conv_one, conv_two):
    local_volume = volume[0]
    cot_flat = cotangent[0]
    depth_len, row_count, col_count = (
        local_volume.shape[1],
        local_volume.shape[2],
        local_volume.shape[3],
    )
    width_one = conv_one.shape[0]
    width_two = conv_two.shape[0]
    weight_one = conv_one.reshape(width_one, -1)
    weight_two = conv_two.reshape(width_two, -1)
    lower_plane = passed_along(local_volume[:, depth_len - 1], "space", 1)
    extended = jnp.concatenate([lower_plane[:, None], local_volume], axis=1)
    padded = jnp.pad(extended, ((0, 0), (0, 0), (1, 0), (1, 0)))
    first_cols = tap_stack(padded, depth_len // 2, row_count // 2, col_count // 2)
    pre_one = jnp.dot(weight_one, first_cols, preferred_element_type=jnp.float32)
    act_one = (
        jax.nn.silu(pre_one)
        .astype(jnp.bfloat16)
        .reshape(width_one, depth_len // 2, row_count // 2, col_count // 2)
    )
    lower_act = passed_along(act_one[:, depth_len // 2 - 1], "space", 1)
    extended_two = jnp.concatenate([lower_act[:, None], act_one], axis=1)
    padded_two = jnp.pad(extended_two, ((0, 0), (0, 0), (1, 0), (1, 0)))
    second_cols = tap_stack(padded_two, depth_len // 4, row_count // 4, col_count // 4)
    out_two = jnp.dot(weight_two, second_cols, preferred_element_type=jnp.float32).astype(
        jnp.bfloat16
    )
    back_cols = jnp.dot(weight_two.T, cot_flat, preferred_element_type=jnp.float32)
    canvas = spread_taps(back_cols, width_one, depth_len // 4, row_count // 4, col_count // 4)
    grad_act = canvas[:, 1:, 1:, 1:]
    upper_part = passed_along(canvas[:, 0, 1:, 1:].astype(jnp.bfloat16), "space", -1).astype(
        jnp.float32
    )
    grad_act = grad_act.at[:, -1].add(upper_part)
    grad_pre = (grad_act.reshape(width_one, -1) * silu_slope(pre_one)).astype(jnp.bfloat16)
    in_one = jnp.dot(first_cols, first_cols.T, preferred_element_type=jnp.float32)
    gram_one = jnp.dot(grad_pre, grad_pre.T, preferred_element_type=jnp.float32)
    grad_one = jnp.dot(grad_pre, first_cols.T, preferred_element_type=jnp.float32)
    in_two = jnp.dot(second_cols, second_cols.T, preferred_element_type=jnp.float32)
    gram_two = jnp.dot(cot_flat, cot_flat.T, preferred_element_type=jnp.float32)
    grad_two = jnp.dot(cot_flat, second_cols.T, preferred_element_type=jnp.float32)
    summed = lax.psum((in_two, in_one, gram_one, grad_one, gram_two, grad_two), ("dp", "space"))
    total_in_two, total_in_one, total_gram_one, total_grad_one, total_gram_two, total_grad_two = (
        summed
    )
    device_count = lax.axis_size("dp") * lax.axis_size("space")
    rows_one = first_cols.shape[1] * device_count
    rows_two = cot_flat.shape[1] * device_count
    step_one, mean_one = precondition(total_in_one, total_gram_one, total_grad_one, rows_one)
    step_two, mean_two = precondition(total_in_two, total_gram_two, total_grad_two, rows_two)
    quad_form = jnp.sum(step_one * mean_one) + jnp.sum(step_two * mean_two)
    factor = jnp.sqrt((step_one.size + step_two.size) / quad_form)
    update_one = (factor * step_one).reshape(-1)
    update_two = (factor * step_two).reshape(-1)
    return (out_two[None], grad_pre[None], update_one, update_two)


def solution(mesh):
    in_specs = (P("dp", None, "space", None, None), P("dp", None, "space"), P(), P())
    out_specs = (P("dp", None, "space"), P("dp", None, "space"), P(), P())
    return jax.shard_map(
        on_device, mesh=mesh, in_specs=in_specs, out_specs=out_specs, check_vma=False
    )
```

profile of v0, /device:TPU:0, one launch (start us, length us, event | category | flops | bytes accessed | tf_op | source)
XLA Modules:
  0.0 933.9 jit_solution(1185647925688393770)
XLA Ops:
  12.8 8.7 scatter_fusion
  21.5 8.7 scatter_fusion.1
  30.3 8.6 scatter_fusion.2
  38.9 8.7 scatter_fusion.3
  47.6 8.7 scatter_fusion.4
  56.3 8.6 scatter_fusion.5
  65.0 8.7 scatter_fusion.6
  73.7 8.7 scatter_fusion.7
  82.4 8.6 scatter_fusion.8
  91.1 8.7 scatter_fusion.9
  99.8 8.7 scatter_fusion.10
  108.5 8.6 scatter_fusion.11
  117.1 8.9 scatter_fusion.12
  126.1 8.7 scatter_fusion.13
  134.8 8.6 scatter_fusion.14
  143.4 8.7 scatter_fusion.15
  152.2 8.7 scatter_fusion.16
  160.9 8.6 scatter_fusion.17
  169.5 8.7 scatter_fusion.18
  178.2 8.7 scatter_fusion.19
  187.0 8.6 scatter_fusion.20
  195.6 8.7 scatter_fusion.21
  204.3 8.7 scatter_fusion.22
  213.0 8.6 scatter_fusion.23
  221.7 9.1 scatter_fusion.24
  230.8 8.7 scatter_fusion.25
  239.6 8.6 scatter_fusion.26
  255.5 5.7 slice.618
  390.8 104.5 %all-reduce.10.cloned.1.call-done = (f32[108,108]{1,0:T(8,128)}, f32[32,108]{1,0:T(8,128)}, f32[32,32]{1,0:T(8,128)}, f32[64,64]{1,0:T(8,128)}) async-done(((f32[108,108]{1,0:T(8,128)}, f32[32,108]{1,0:T(8,128)}, f32[32,32]{1,0:T(8,128)}, f32[64,64]{1,0:T(8,128)}), (f32[108,108]{1,0:T(8,128)}, f32[32,108]{1,0:T(8,128)}, f32[32,32]{1,0:T(8,128)}, f32[64,64]{1,0:T(8,128)})) %all-reduce.10.cloned.1.call-update) | async-done | bytes 80976 | tf_op jit(solution)/shard_map/psum | solution.py:112
  497.0 9.9 %cholesky.246 = f32[108,108]{1,0:T(8,128)S(1)} custom-call(f32[108,108]{1,0:T(8,128)S(1)} %fusion.98), custom_call_target="Cholesky" | custom-call | tf_op jit(solution)/shard_map/jit(cholesky)/cholesky | solution.py:57
  514.8 8.3 custom-call.89
  526.4 5.8 cholesky.255
  542.7 97.4 %all-reduce.12.cloned.1.call-done = (f32[864,864]{1,0:T(8,128)}, f32[64,864]{1,0:T(8,128)}) async-done(((f32[864,864]{1,0:T(8,128)}, f32[64,864]{1,0:T(8,128)}), (f32[864,864]{1,0:T(8,128)}, f32[64,864]{1,0:T(8,128)})) %all-reduce.12.cloned.1.call-update) | async-done | bytes 3207184 | tf_op jit(solution)/shard_map/psum | solution.py:112
  652.4 11.7 %cholesky.269 = f32[128,128]{1,0:T(8,128)S(1)} custom-call(f32[128,128]{1,0:T(8,128)S(1)} %cholesky.607), custom_call_target="Cholesky" | custom-call | tf_op jit(solution)/shard_map/jit(cholesky)/cholesky | solution.py:57
  665.1 9.8 %custom-call.91 = f32[1,128,128]{1,2,0:T(8,128)S(1)} custom-call(f32[1,128,128]{2,1,0:T(8,128)S(1)} %get-tuple-element.85), custom_call_target="InvertDiagBlocksLowerTriangular" | custom-call | tf_op jit(solution)/shard_map/jit(cholesky)/cholesky | solution.py:57
  678.4 12.5 %cholesky.492 = f32[128,128]{1,0:T(8,128)S(1)} custom-call(f32[128,128]{1,0:T(8,128)} %cholesky.611), custom_call_target="Cholesky" | custom-call | tf_op jit(solution)/shard_map/jit(cholesky)/cholesky | solution.py:57
  691.6 11.0 %custom-call.92 = f32[1,128,128]{1,2,0:T(8,128)S(1)} custom-call(f32[1,128,128]{2,1,0:T(8,128)} %get-tuple-element.82), custom_call_target="InvertDiagBlocksLowerTriangular" | custom-call | tf_op jit(solution)/shard_map/jit(cholesky)/cholesky | solution.py:57
  704.7 11.7 %cholesky.513 = f32[128,128]{1,0:T(8,128)S(1)} custom-call(f32[128,128]{1,0:T(8,128)S(1)} %cholesky.616), custom_call_target="Cholesky" | custom-call | tf_op jit(solution)/shard_map/jit(cholesky)/cholesky | solution.py:57
  716.5 9.8 %custom-call.93 = f32[1,128,128]{1,2,0:T(8,128)S(1)} custom-call(f32[1,128,128]{2,1,0:T(8,128)S(1)} %get-tuple-element.79), custom_call_target="InvertDiagBlocksLowerTriangular" | custom-call | tf_op jit(solution)/shard_map/jit(cholesky)/cholesky | solution.py:57
  728.3 11.9 %cholesky.532 = f32[128,128]{1,0:T(8,128)S(1)} custom-call(f32[128,128]{1,0:T(8,128)S(1)} %cholesky.621), custom_call_target="Cholesky" | custom-call | tf_op jit(solution)/shard_map/jit(cholesky)/cholesky | solution.py:57
  740.2 9.8 %custom-call.94 = f32[1,128,128]{1,2,0:T(8,128)S(1)} custom-call(f32[1,128,128]{2,1,0:T(8,128)S(1)} %get-tuple-element.76), custom_call_target="InvertDiagBlocksLowerTriangular" | custom-call | tf_op jit(solution)/shard_map/jit(cholesky)/cholesky | solution.py:57
  752.0 11.7 %cholesky.551 = f32[128,128]{1,0:T(8,128)S(1)} custom-call(f32[128,128]{1,0:T(8,128)S(1)} %cholesky.626), custom_call_target="Cholesky" | custom-call | tf_op jit(solution)/shard_map/jit(cholesky)/cholesky | solution.py:57
  763.8 9.8 %custom-call.95 = f32[1,128,128]{1,2,0:T(8,128)S(1)} custom-call(f32[1,128,128]{2,1,0:T(8,128)S(1)} %get-tuple-element.73), custom_call_target="InvertDiagBlocksLowerTriangular" | custom-call | tf_op jit(solution)/shard_map/jit(cholesky)/cholesky | solution.py:57
  775.4 11.9 %cholesky.571 = f32[128,128]{1,0:T(8,128)S(1)} custom-call(f32[128,128]{1,0:T(8,128)S(1)} %cholesky.631), custom_call_target="Cholesky" | custom-call | tf_op jit(solution)/shard_map/jit(cholesky)/cholesky | solution.py:57
  787.4 9.8 %custom-call.96 = f32[1,128,128]{1,2,0:T(8,128)S(1)} custom-call(f32[1,128,128]{2,1,0:T(8,128)S(1)} %get-tuple-element.70), custom_call_target="InvertDiagBlocksLowerTriangular" | custom-call | tf_op jit(solution)/shard_map/jit(cholesky)/cholesky | solution.py:57
  798.6 8.8 cholesky.592
  818.4 18.1 %while.2 = (s32[]{:T(128)}, f32[864,864]{1,0:T(8,128)}, s32[6,2]{0,1:T(2,128)S(1)}, f32[6,128,128]{2,1,0:T(8,128)S(1)}, s32[]{:T(128)}) while((s32[]{:T(128)}, f32[864,864]{1,0:T(8,128)}, s32[6,2]{0,1:T(2,128)S(1)}, f32[6,128,128]{2,1,0:T(8,128)S(1)}, s32[]{:T(128)}) %tuple.123), condition=%wide.while_cond.1, body=%wide.while_body.1.sunk | while | flops 2 | bytes 131189 | solution.py:58
  838.4 69.8 %custom-call.97 = f32[7,128,128]{1,2,0:T(8,128)S(1)} custom-call(f32[7,128,128]{2,1,0:T(8,128)} %pad_maximum_fusion), custom_call_target="InvertDiagBlocksLowerTriangular" | custom-call | tf_op jit(solution)/shard_map/jit(_cho_solve)/triangular_solve | solution.py:58
  (350 shorter events, 235.0 us)
Async XLA Ops:
  7.2 488.1 %all-reduce.10.cloned.1.call-start = ((), (), s32[]{:S(2)}) async-start(), calls=%async_computation | async-start | bytes 245760 | tf_op jit(solution)/shard_map/psum | solution.py:112
  239.5 10.6 %copy-start.8 = (bf16[1,4,8,32,32]{4,3,2,1,0:T(8,128)(2,1)S(1)}, bf16[1,4,8,32,32]{4,3,2,1,0:T(8,128)(2,1)}, u32[]{:S(2)}) copy-start(bf16[1,4,8,32,32]{4,3,2,1,0:T(8,128)(2,1)} %param.6) | copy-start | bytes 196612
  239.5 13.7 %copy-start.10 = (bf16[1,64,128]{2,1,0:T(8,128)(2,1)S(1)}, bf16[1,64,128]{2,1,0:T(8,128)(2,1)}, u32[]{:S(2)}) copy-start(bf16[1,64,128]{2,1,0:T(8,128)(2,1)} %param.7) | copy-start | bytes 49156
  239.5 15.7 %copy-start.12 = (bf16[32,4,3,3,3]{0,1,4,3,2:T(4,128)(2,1)S(1)}, bf16[32,4,3,3,3]{0,1,4,3,2:T(4,128)(2,1)}, u32[]{:S(2)}) copy-start(bf16[32,4,3,3,3]{0,1,4,3,2:T(4,128)(2,1)} %param.8) | copy-start | bytes 20740
  248.8 112.8 %collective-permute-start.2 = (bf16[32,16,16]{0,2,1:T(8,128)(2,1)}, bf16[32,16,16]{0,2,1:T(8,128)(2,1)}, u32[]{:S(2)}, u32[]{:S(2)}) collective-permute-start(bf16[32,16,16]{0,2,1:T(8,128)(2,1)} %fusion.66), channel_id=1, source_target_pairs={{1,0},{2,1},{3,2},{5,4},{6,5},{7,6},{9,8},{10,9},{11,10},{13,12},{... | collective-permute-start | bytes 49160 | tf_op jit(solution)/shard_map/ppermute | solution.py:13
  250.2 5.1 collective-permute-start
  362.8 20.5 %copy-start.4 = (bf16[32,1024]{1,0:T(8,128)(2,1)}, bf16[32,1024]{1,0:T(8,128)(2,1)S(1)}, u32[]{:S(2)}) copy-start(bf16[32,1024]{1,0:T(8,128)(2,1)S(1)} %get-tuple-element.67) | copy-start | bytes 196612
  363.0 6.1 collective-permute-start.1
  369.0 271.0 %all-reduce.12.cloned.1.call-start = ((), (), s32[]{:S(2)}) async-start(), calls=%async_computation.1 | async-start | bytes 6651904 | tf_op jit(solution)/shard_map/psum | solution.py:112
  643.9 4.6 copy-start
  650.8 1.6 copy-start.3
  652.4 12.0 %copy-start.5 = (f32[64,864]{1,0:T(8,128)S(1)}, f32[64,864]{1,0:T(8,128)}, u32[]{:S(2)}) copy-start(f32[64,864]{1,0:T(8,128)} %get-tuple-element.37) | copy-start | bytes 663556
  816.4 0.9 copy-start.13
  816.4 1.9 copy-start.7
  816.5 20.1 %copy-start.9 = (f32[128,32]{1,0:T(8,128)S(1)}, f32[128,32]{1,0:T(8,128)}, u32[]{:S(2)}) copy-start(f32[128,32]{1,0:T(8,128)} %pad_convert_fusion) | copy-start | bytes 49156
  816.7 1.7 copy-start.1
  836.5 78.4 %copy-start.2 = (f32[864,864]{1,0:T(8,128)S(1)}, f32[864,864]{1,0:T(8,128)}, u32[]{:S(2)}) copy-start(f32[864,864]{1,0:T(8,128)} %get-tuple-element.214) | copy-start | bytes 8957956
  913.3 8.2 copy-start.11
  914.9 7.1 copy-start.6
Sparse Core Ops, SparseCore 0:
  369.2 126.0 all-reduce.9
  500.9 139.1 all-reduce.11
where the time goes:
time: 946 us; the launch traced here: 934 us
  other arithmetic  507 us (54%)
  waiting for transfers between devices  202 us (21%)
  local copies, waits for them, and re-layouts  157 us (17%)
  matrix products  37.8 us (4%)
  between operations  22.1 us (2%)
    scatter-add x27, other arithmetic, spread_taps(): canvas = canvas.at[:, depth_tap:depth_tap + 2 * out_depth:2, row_tap:row_...  235 us
    psum x2, waiting for transfers between devices, on_device(): lax.psum((in_two, in_one, gram_one, grad_one, gram_two, grad_two), ('dp',...  202 us
    another operation x36, other arithmetic, damped_solve(): lower_factor = jnp.linalg.cholesky(matrix)  166 us
    another operation x13, other arithmetic, damped_solve(): return jax.scipy.linalg.cho_solve((lower_factor, True), rhs_terms)  91.3 us
    slice x54, local copies, waits for them, and re-layouts, tap_stack(): padded[:, depth_tap:depth_tap + 2 * out_depth:2, row_tap:row_tap + 2 * ou...  90.9 us
    unnamed x95, local copies, waits for them, and re-layouts  27 us
  transfers between devices with their start and end apart: 5, of which 2 were waited for; matrix products, arithmetic and copies ran while one was open for 19% of the time, Pallas kernels for 0%

commit v1 on v0

--- a/solution.py
+++ b/solution.py
@@ -109,7 +109,8 @@
     in_two = jnp.dot(second_cols, second_cols.T, preferred_element_type=jnp.float32)
     gram_two = jnp.dot(cot_flat, cot_flat.T, preferred_element_type=jnp.float32)
     grad_two = jnp.dot(cot_flat, second_cols.T, preferred_element_type=jnp.float32)
-    summed = lax.psum((in_two, in_one, gram_one, grad_one, gram_two, grad_two), ("dp", "space"))
+    val = jax.lax.psum((in_two, in_one, gram_one, grad_one, gram_two, grad_two), axis_name="dp")
+    summed = jax.lax.psum(val, axis_name="space")
     total_in_two, total_in_one, total_gram_one, total_grad_one, total_gram_two, total_grad_two = (
         summed
     )

time: 946 us -> 996 us (1.053)
  waiting for transfers between devices: 202 us -> 250 us
    psum x2 -> x4, waiting for transfers between devices: 202 us -> 250 us  [the longest x2 172 us: on_device(): jax.lax.psum((in_two, in_one, gram_one, grad_one, gram_two, grad_two), ax...]
    unnamed x95 -> x97, local copies, waits for them, and re-layouts: 27 us -> 27.1 us
  transfers between devices with their start and end apart: 5 -> 7, of which waited for: 2 -> 4; matrix products, arithmetic and copies ran while one was open for 19% -> 18% of each run, Pallas kernels for 0% -> 0%
where the time goes in v1:
time: 996 us; the launch traced here: 985 us
  other arithmetic  510 us (51%)
  waiting for transfers between devices  250 us (25%)
  local copies, waits for them, and re-layouts  157 us (16%)
  matrix products  37.2 us (4%)
  between operations  21.5 us (2%)
    scatter-add x27, other arithmetic, spread_taps(): canvas = canvas.at[:, depth_tap:depth_tap + 2 * out_depth:2, row_tap:row_...  235 us
    psum x2, waiting for transfers between devices, on_device(): jax.lax.psum((in_two, in_one, gram_one, grad_one, gram_two, grad_two), ax...  172 us
    another operation x36, other arithmetic, damped_solve(): lower_factor = jnp.linalg.cholesky(matrix)  171 us
    slice x54, local copies, waits for them, and re-layouts, tap_stack(): padded[:, depth_tap:depth_tap + 2 * out_depth:2, row_tap:row_tap + 2 * ou...  91 us
    another operation x13, other arithmetic, damped_solve(): return jax.scipy.linalg.cho_solve((lower_factor, True), rhs_terms)  90.6 us
    psum x2, waiting for transfers between devices, on_device(): summed = jax.lax.psum(val, axis_name='space')  77.7 us
    unnamed x97, local copies, waits for them, and re-layouts  27.1 us
  transfers between devices with their start and end apart: 7, of which 4 were waited for; matrix products, arithmetic and copies ran while one was open for 18% of the time, Pallas kernels for 0%

profile of v1, /device:TPU:0, one launch (start us, length us, event | category | flops | bytes accessed | tf_op | source)
XLA Modules:
  0.0 984.6 jit_solution(5324492522883427069)
XLA Ops:
  12.8 8.7 scatter_fusion
  21.5 8.7 scatter_fusion.1
  30.3 8.6 scatter_fusion.2
  38.9 8.7 scatter_fusion.3
  47.6 8.7 scatter_fusion.4
  56.3 8.6 scatter_fusion.5
  65.0 8.7 scatter_fusion.6
  73.7 8.7 scatter_fusion.7
  82.4 8.6 scatter_fusion.8
  91.1 8.7 scatter_fusion.9
  99.8 8.7 scatter_fusion.10
  108.5 8.6 scatter_fusion.11
  117.1 9.2 scatter_fusion.12
  126.3 8.7 scatter_fusion.13
  135.0 8.6 scatter_fusion.14
  143.7 8.7 scatter_fusion.15
  152.4 8.7 scatter_fusion.16
  161.1 8.6 scatter_fusion.17
  169.8 8.7 scatter_fusion.18
  178.5 8.7 scatter_fusion.19
  187.2 8.6 scatter_fusion.20
  195.9 8.7 scatter_fusion.21
  204.6 8.7 scatter_fusion.22
  213.3 8.6 scatter_fusion.23
  221.9 8.9 scatter_fusion.24
  230.8 8.7 scatter_fusion.25
  239.6 8.6 scatter_fusion.26
  387.8 52.9 %all-reduce.14.cloned.1.call-done = (f32[108,108]{1,0:T(8,128)}, f32[32,108]{1,0:T(8,128)}, f32[32,32]{1,0:T(8,128)}, f32[64,64]{1,0:T(8,128)}) async-done(((f32[108,108]{1,0:T(8,128)}, f32[32,108]{1,0:T(8,128)}, f32[32,32]{1,0:T(8,128)}, f32[64,64]{1,0:T(8,128)}), (f32[108,108]{1,0:T(8,128)}, f32[32,108]{1,0:T(8,128)}, f32[32,32]{1,0:T(8,128)}, f32[64,64]{1,0:T(8,128)})) %all-reduce.14.cloned.1.call-update) | async-done | bytes 80976 | tf_op jit(solution)/shard_map/psum | solution.py:112
  443.3 31.1 %all-reduce.18.cloned.1.call-done = (f32[108,108]{1,0:T(8,128)}, f32[32,108]{1,0:T(8,128)}, f32[32,32]{1,0:T(8,128)}, f32[64,64]{1,0:T(8,128)}) async-done(((f32[108,108]{1,0:T(8,128)}, f32[32,108]{1,0:T(8,128)}, f32[32,32]{1,0:T(8,128)}, f32[64,64]{1,0:T(8,128)}), (f32[108,108]{1,0:T(8,128)}, f32[32,108]{1,0:T(8,128)}, f32[32,32]{1,0:T(8,128)}, f32[64,64]{1,0:T(8,128)})) %all-reduce.18.cloned.1.call-update) | async-done | bytes 80976 | tf_op jit(solution)/shard_map/psum | solution.py:113
  476.2 9.9 %cholesky.246 = f32[108,108]{1,0:T(8,128)S(1)} custom-call(f32[108,108]{1,0:T(8,128)S(1)} %fusion.98), custom_call_target="Cholesky" | custom-call | tf_op jit(solution)/shard_map/jit(cholesky)/cholesky | solution.py:57
  493.3 118.9 %all-reduce.16.cloned.1.call-done = (f32[864,864]{1,0:T(8,128)}, f32[64,864]{1,0:T(8,128)}) async-done(((f32[864,864]{1,0:T(8,128)}, f32[64,864]{1,0:T(8,128)}), (f32[864,864]{1,0:T(8,128)}, f32[64,864]{1,0:T(8,128)})) %all-reduce.16.cloned.1.call-update) | async-done | bytes 3207184 | tf_op jit(solution)/shard_map/psum | solution.py:112
  612.9 8.3 custom-call.89
  638.6 46.6 %all-reduce.20.cloned.1.call-done = (f32[864,864]{1,0:T(8,128)}, f32[64,864]{1,0:T(8,128)}) async-done(((f32[864,864]{1,0:T(8,128)}, f32[64,864]{1,0:T(8,128)}), (f32[864,864]{1,0:T(8,128)}, f32[64,864]{1,0:T(8,128)})) %all-reduce.20.cloned.1.call-update) | async-done | bytes 3207184 | tf_op jit(solution)/shard_map/psum | solution.py:113
  697.8 11.7 %cholesky.269 = f32[128,128]{1,0:T(8,128)S(1)} custom-call(f32[128,128]{1,0:T(8,128)S(1)} %cholesky.607), custom_call_target="Cholesky" | custom-call | tf_op jit(solution)/shard_map/jit(cholesky)/cholesky | solution.py:57
  710.4 9.8 custom-call.91
  723.8 13.2 %cholesky.492 = f32[128,128]{1,0:T(8,128)} custom-call(f32[128,128]{1,0:T(8,128)} %cholesky.611), custom_call_target="Cholesky" | custom-call | tf_op jit(solution)/shard_map/jit(cholesky)/cholesky | solution.py:57
  738.5 11.4 %custom-call.92 = f32[1,128,128]{1,2,0:T(8,128)} custom-call(f32[1,128,128]{2,1,0:T(8,128)} %get-tuple-element.88), custom_call_target="InvertDiagBlocksLowerTriangular" | custom-call | tf_op jit(solution)/shard_map/jit(cholesky)/cholesky | solution.py:57
  753.4 12.5 %cholesky.513 = f32[128,128]{1,0:T(8,128)S(1)} custom-call(f32[128,128]{1,0:T(8,128)} %cholesky.616), custom_call_target="Cholesky" | custom-call | tf_op jit(solution)/shard_map/jit(cholesky)/cholesky | solution.py:57
  766.6 10.6 %custom-call.93 = f32[1,128,128]{1,2,0:T(8,128)S(1)} custom-call(f32[1,128,128]{2,1,0:T(8,128)} %get-tuple-element.85), custom_call_target="InvertDiagBlocksLowerTriangular" | custom-call | tf_op jit(solution)/shard_map/jit(cholesky)/cholesky | solution.py:57
  779.3 11.9 %cholesky.532 = f32[128,128]{1,0:T(8,128)S(1)} custom-call(f32[128,128]{1,0:T(8,128)S(1)} %cholesky.621), custom_call_target="Cholesky" | custom-call | tf_op jit(solution)/shard_map/jit(cholesky)/cholesky | solution.py:57
  791.3 9.8 custom-call.94
  803.1 11.7 %cholesky.551 = f32[128,128]{1,0:T(8,128)S(1)} custom-call(f32[128,128]{1,0:T(8,128)S(1)} %cholesky.626), custom_call_target="Cholesky" | custom-call | tf_op jit(solution)/shard_map/jit(cholesky)/cholesky | solution.py:57
  814.8 9.8 custom-call.95
  826.4 12.1 %cholesky.571 = f32[128,128]{1,0:T(8,128)S(1)} custom-call(f32[128,128]{1,0:T(8,128)S(1)} %cholesky.631), custom_call_target="Cholesky" | custom-call | tf_op jit(solution)/shard_map/jit(cholesky)/cholesky | solution.py:57
  838.6 9.8 custom-call.96
  849.8 8.8 cholesky.592
  869.5 18.3 %while.2 = (s32[]{:T(128)}, f32[864,864]{1,0:T(8,128)}, s32[6,2]{0,1:T(2,128)S(1)}, f32[6,128,128]{2,1,0:T(8,128)S(1)}, s32[]{:T(128)}) while((s32[]{:T(128)}, f32[864,864]{1,0:T(8,128)}, s32[6,2]{0,1:T(2,128)S(1)}, f32[6,128,128]{2,1,0:T(8,128)S(1)}, s32[]{:T(128)}) %tuple.129), condition=%wide.while_cond.1, body=%wide.while_body.1.sunk | while | flops 2 | bytes 131189 | solution.py:58
  889.7 69.7 %custom-call.97 = f32[7,128,128]{1,2,0:T(8,128)S(1)} custom-call(f32[7,128,128]{2,1,0:T(8,128)} %pad_maximum_fusion), custom_call_target="InvertDiagBlocksLowerTriangular" | custom-call | tf_op jit(solution)/shard_map/jit(_cho_solve)/triangular_solve | solution.py:58
  (358 shorter events, 247.2 us)
Async XLA Ops:
  7.2 433.5 %all-reduce.14.cloned.1.call-start = ((), (), s32[]{:S(2)}) async-start(), calls=%async_computation | async-start | bytes 245760 | tf_op jit(solution)/shard_map/psum | solution.py:112
  239.5 10.6 %copy-start.8 = (bf16[1,4,8,32,32]{4,3,2,1,0:T(8,128)(2,1)S(1)}, bf16[1,4,8,32,32]{4,3,2,1,0:T(8,128)(2,1)}, u32[]{:S(2)}) copy-start(bf16[1,4,8,32,32]{4,3,2,1,0:T(8,128)(2,1)} %param.6) | copy-start | bytes 196612
  239.6 13.7 %copy-start.9 = (bf16[1,64,128]{2,1,0:T(8,128)(2,1)S(1)}, bf16[1,64,128]{2,1,0:T(8,128)(2,1)}, u32[]{:S(2)}) copy-start(bf16[1,64,128]{2,1,0:T(8,128)(2,1)} %param.7) | copy-start | bytes 49156
  239.6 14.5 %copy-start.13 = (bf16[32,4,3,3,3]{0,1,4,3,2:T(4,128)(2,1)S(1)}, bf16[32,4,3,3,3]{0,1,4,3,2:T(4,128)(2,1)}, u32[]{:S(2)}) copy-start(bf16[32,4,3,3,3]{0,1,4,3,2:T(4,128)(2,1)} %param.8) | copy-start | bytes 20740
  248.9 111.6 %collective-permute-start.2 = (bf16[32,16,16]{0,2,1:T(8,128)(2,1)}, bf16[32,16,16]{0,2,1:T(8,128)(2,1)}, u32[]{:S(2)}, u32[]{:S(2)}) collective-permute-start(bf16[32,16,16]{0,2,1:T(8,128)(2,1)} %fusion.66), channel_id=1, source_target_pairs={{1,0},{2,1},{3,2},{5,4},{6,5},{7,6},{9,8},{10,9},{11,10},{13,12},{... | collective-permute-start | bytes 49160 | tf_op jit(solution)/shard_map/ppermute | solution.py:13
  250.2 3.9 collective-permute-start
  361.6 20.6 %copy-start.4 = (bf16[32,1024]{1,0:T(8,128)(2,1)}, bf16[32,1024]{1,0:T(8,128)(2,1)S(1)}, u32[]{:S(2)}) copy-start(bf16[32,1024]{1,0:T(8,128)(2,1)S(1)} %get-tuple-element.73) | copy-start | bytes 196612
  361.8 6.2 collective-permute-start.1
  368.0 106.4 %all-reduce.18.cloned.1.call-start = ((), (), s32[]{:S(2)}) async-start(), calls=%async_computation.2 | async-start | bytes 245760 | tf_op jit(solution)/shard_map/psum | solution.py:113
  440.7 171.5 %all-reduce.16.cloned.1.call-start = ((), (), s32[]{:S(2)}) async-start(), calls=%async_computation.1 | async-start | bytes 6651904 | tf_op jit(solution)/shard_map/psum | solution.py:112
  441.6 243.6 %all-reduce.20.cloned.1.call-start = ((), (), s32[]{:S(2)}) async-start(), calls=%async_computation.3 | async-start | bytes 6651904 | tf_op jit(solution)/shard_map/psum | solution.py:113
  474.4 149.4 %copy-start.10 = (f32[64,64]{1,0:T(8,128)S(1)}, f32[64,64]{1,0:T(8,128)}, u32[]{:S(2)}) copy-start(f32[64,64]{1,0:T(8,128)} %get-tuple-element.41) | copy-start | bytes 49156
  474.4 162.1 %copy-start.12 = (f32[32,108]{1,0:T(8,128)S(1)}, f32[32,108]{1,0:T(8,128)}, u32[]{:S(2)}) copy-start(f32[32,108]{1,0:T(8,128)} %get-tuple-element.39) | copy-start | bytes 41476
  689.0 4.8 copy-start
  696.1 1.6 copy-start.3
  697.8 12.0 %copy-start.5 = (f32[64,864]{1,0:T(8,128)S(1)}, f32[64,864]{1,0:T(8,128)}, u32[]{:S(2)}) copy-start(f32[64,864]{1,0:T(8,128)} %get-tuple-element.43) | copy-start | bytes 663556
  867.6 0.9 copy-start.14
  867.6 1.9 copy-start.7
  867.9 1.7 copy-start.1
  887.8 78.3 %copy-start.2 = (f32[864,864]{1,0:T(8,128)S(1)}, f32[864,864]{1,0:T(8,128)}, u32[]{:S(2)}) copy-start(f32[864,864]{1,0:T(8,128)} %get-tuple-element.232) | copy-start | bytes 8957956
  964.6 8.2 copy-start.11
  966.2 7.1 copy-start.6
Sparse Core Ops, SparseCore 0:
  368.1 72.5 all-reduce.13
  443.2 31.1 all-reduce.17
  478.1 134.1 all-reduce.15
  614.5 70.6 all-reduce.19
